TPU v7x, 32 devices: a whole 2x2x4 slice. The times are simulated.
32 devices in a mesh: parts: 2 (over y), tm: 4 (over z), rows: 2 (over x), cols: 2 (over core).
Axes of the slice: x: 2, y: 2, z: 4, core: 2. Of those that a mesh axis runs over, the one named last changes fastest.
Arguments:
- frames: bfloat16 [256, 256, 512], P(('parts', 'tm'), 'rows', 'cols'), parts along dimension 0, may hold values from -6 to 6
- transfer: bfloat16 [256, 128, 128], P(('parts', 'tm')), parts along dimension 0, may hold values from 0.099609375 to 1
- cutoff: int32 [128, 128], replicated, may hold values from 0 to 64
Outputs:
- restored: float32 [256, 256, 512], P(('parts', 'tm'), 'rows', 'cols'), parts along dimension 0
There are 2 independent parts, one for each index of `parts`. A program takes and returns all parts, laid end to end along the dimension named above; an argument that names none is the same for every part. Nothing has to cross between parts.
Inputs may be any that keep to these rules, and one draw needn't show every extreme that they name: cutoff[u, v] is the largest value of min(w, 128 - w) kept at wavenumber (u, v).
All inputs are finite; a program needn't handle non-finite values.
Results may differ from a plain program's by a relative error of at most 0.0003.
Values may be sent and summed in bfloat16 or wider, within the bound.
No kernel may reach another device: no remote copies, remote signals or barrier semaphores. Data moves between devices by JAX's collectives and lax.ppermute only.
A program may use at most 128 MiB of HBM per device.

v0:
```python
import math

import jax
import jax.numpy as jnp
from jax import lax
from jax.sharding import PartitionSpec as P

noise_level = 0.05


def with_halo(cells, sides, width):
    for axis, dim in sides:
        count = lax.axis_size(axis)
        ends = count - 1
        head = lax.slice_in_dim(cells, 0, width, axis=dim)
        tail = lax.slice_in_dim(cells, cells.shape[dim] - width, cells.shape[dim], axis=dim)
        cells = jnp.concatenate(
            [
                lax.ppermute(tail, axis, [(i, (i + 1) % count) for i in range(ends)]),
                cells,
                lax.ppermute(head, axis, [((i + 1) % count, i) for i in range(ends)]),
            ],
            axis=dim,
        )
    return cells


def tables(length):
    series = jnp.arange(length, dtype=jnp.int32)
    product = series[:, None] * series[None, :] % length
    angles = product.astype(jnp.float32) * (2.0 * math.pi / length)
    return (jnp.cos(angles), jnp.sin(angles))


def forward_spatial(images, cos_space, sin_space):
    highest = lax.Precision.HIGHEST
    factor = 1.0 / cos_space.shape[0]
    row_real = jnp.einsum("cnab,bv->cnav", images, cos_space, precision=highest)
    row_imag = -jnp.einsum("cnab,bv->cnav", images, sin_space, precision=highest)
    spec_real = (
        jnp.einsum("ua,cnav->cnuv", cos_space, row_real, precision=highest)
        + jnp.einsum("ua,cnav->cnuv", sin_space, row_imag, precision=highest)
    ) * factor
    spec_imag = (
        jnp.einsum("ua,cnav->cnuv", cos_space, row_imag, precision=highest)
        - jnp.einsum("ua,cnav->cnuv", sin_space, row_real, precision=highest)
    ) * factor
    return (spec_real, spec_imag)


def inverse_spatial(spec_real, spec_imag, cos_space, sin_space):
    highest = lax.Precision.HIGHEST
    factor = 1.0 / cos_space.shape[0]
    col_real = jnp.einsum("au,cnuv->cnav", cos_space, spec_real, precision=highest) - jnp.einsum(
        "au,cnuv->cnav", sin_space, spec_imag, precision=highest
    )
    col_imag = jnp.einsum("au,cnuv->cnav", cos_space, spec_imag, precision=highest) + jnp.einsum(
        "au,cnuv->cnav", sin_space, spec_real, precision=highest
    )
    return (
        jnp.einsum("cnav,vb->cnab", col_real, cos_space, precision=highest)
        - jnp.einsum("cnav,vb->cnab", col_imag, sin_space, precision=highest)
    ) * factor


def join(spec_real, spec_imag, gains, count):
    numerator_real = jnp.zeros(spec_real.shape[:1] + (count,) + spec_real.shape[2:], jnp.float32)
    numerator_imag = jnp.zeros_like(numerator_real)
    denominator = jnp.zeros(gains.shape[:1] + (count,) + gains.shape[2:], jnp.float32)
    for offset in range(5):
        gain = lax.slice_in_dim(gains, offset, offset + count, axis=1)
        numerator_real = numerator_real + gain * lax.slice_in_dim(
            spec_real, offset, offset + count, axis=1
        )
        numerator_imag = numerator_imag + gain * lax.slice_in_dim(
            spec_imag, offset, offset + count, axis=1
        )
        denominator = denominator + gain * gain
    denominator = denominator + noise_level
    return (numerator_real / denominator, numerator_imag / denominator)


def temporal(stacked, cutoff_local, channels):
    highest = lax.Precision.HIGHEST
    time_len = stacked.shape[1]
    cos_time, sin_time = tables(time_len)
    factor = 1.0 / math.sqrt(time_len)
    real = stacked[:channels]
    imag = stacked[channels:]
    freq_real = (
        jnp.einsum("wt,stk->swk", cos_time, real, precision=highest)
        + jnp.einsum("wt,stk->swk", sin_time, imag, precision=highest)
    ) * factor
    freq_imag = (
        jnp.einsum("wt,stk->swk", cos_time, imag, precision=highest)
        - jnp.einsum("wt,stk->swk", sin_time, real, precision=highest)
    ) * factor
    omega = jnp.arange(time_len, dtype=jnp.int32)
    distance = jnp.minimum(omega, time_len - omega)
    keeper = (distance[:, None] <= cutoff_local[None, :])[None]
    freq_real = jnp.where(keeper, freq_real, 0.0)
    freq_imag = jnp.where(keeper, freq_imag, 0.0)
    back_real = (
        jnp.einsum("tw,swk->stk", cos_time, freq_real, precision=highest)
        - jnp.einsum("tw,swk->stk", sin_time, freq_imag, precision=highest)
    ) * factor
    back_imag = (
        jnp.einsum("tw,swk->stk", cos_time, freq_imag, precision=highest)
        + jnp.einsum("tw,swk->stk", sin_time, freq_real, precision=highest)
    ) * factor
    return jnp.concatenate([back_real, back_imag], axis=0)


def to_channels(images, side, across):
    total = images.shape[0]
    return images.reshape(total, side, across, side).transpose(2, 0, 1, 3)


def on_device(frames, transfer, cutoff):
    count = frames.shape[0]
    side = transfer.shape[1]
    across = frames.shape[2] // side
    cos_space, sin_space = tables(side)
    packed = jnp.concatenate([frames, transfer], axis=2)
    extended = with_halo(packed, (("tm", 0),), 2)
    images = to_channels(extended[:, :, : across * side].astype(jnp.float32), side, across)
    spec_real, spec_imag = forward_spatial(images, cos_space, sin_space)
    gains = extended[:, :, across * side :].astype(jnp.float32)[None]
    joined_real, joined_imag = join(spec_real, spec_imag, gains, count)
    payload = jnp.concatenate([joined_real, joined_imag], axis=0).reshape(
        2 * across, count, side * side
    )
    gathered = lax.all_to_all(payload, "tm", split_axis=2, concat_axis=1, tiled=True)
    width = gathered.shape[2]
    start = lax.axis_index("tm") * width
    cutoff_local = lax.dynamic_slice_in_dim(cutoff.reshape(-1), start, width)
    filtered = temporal(gathered, cutoff_local, across)
    returned = lax.all_to_all(filtered, "tm", split_axis=1, concat_axis=2, tiled=True)
    spectra_back = returned.reshape(2 * across, count, side, side)
    result = inverse_spatial(spectra_back[:across], spectra_back[across:], cos_space, sin_space)
    return result.transpose(1, 2, 0, 3).reshape(count, side, across * side)


def solution(mesh):
    return jax.shard_map(
        on_device,
        mesh=mesh,
        in_specs=(P(("parts", "tm"), "rows", "cols"), P(("parts", "tm"), None, None), P()),
        out_specs=P(("parts", "tm"), "rows", "cols"),
        check_vma=False,
    )
```

profile of v0, /device:TPU:13, one launch (start us, length us, event | category | flops | bytes accessed | tf_op | source)
XLA Modules:
  0.0 774.3 jit_solution(10579485411199657045)
XLA Ops:
  0.0 3.2 copy.61
  3.2 2.2 copy.62
  5.5 3.2 collective-permute-start
  10.8 2.4 collective-permute-done
  13.2 2.9 collective-permute-done.1
  17.7 3.0 copy.63
  20.8 2.3 fusion.30
  25.3 7.9 %fusion.10 = f32[2,36,128,128]{3,2,1,0:T(8,128)S(1)} fusion(f32[2,36,128,128]{3,2,1,0:T(8,128)S(1)} %fusion.30), kind=kOutput, calls=%fused_computation.18 | convolution fusion | flops 1813348352 | bytes 9437184 | tf_op jit(solution)/shard_map/ua,cnav->cnuv/dot_general | solution.py:45
  33.2 7.7 fusion.12
  40.9 4.8 multiply_bitcast_fusion
  45.7 4.4 multiply_bitcast_fusion.1
  51.8 11.6 %slice_bitcast_fusion.4 = (f32[32,128,128]{1,2,0:T(8,128)}, f32[32,128,128]{1,2,0:T(8,128)}, f32[32,128,128]{1,2,0:T(8,128)}, f32[32,128,128]{1,2,0:T(8,128)}, f...) fusion(f32[1,36,128,128]{2,3,1,0:T(8,128)} %fusion.36), kind=kLoop, calls=%fused_computation.61 | loop fusion | flops 5242880 | bytes 23068672 | tf_op jit(solution)/shard_map/mul | solution.py:72
  63.3 9.8 %fusion.20 = (f32[2,32,128,128]{2,3,1,0:T(8,128)S(1)}, f32[2,32,128,128]{2,3,1,0:T(8,128)}) fusion(f32[2,36,128,128]{2,3,1,0:T(8,128)S(1)} %multiply_bitcast_fusion.1, f32[32,128,128]{1,2,0:T(8,128)} %get-tuple-element.14, f32[32,128,128]{1,2,0:T(8,128)} %get-tuple-element.15, f32[32,128,128]{1,2,0:T(8,128)} %get-tuple-element.16, ...), kind=kLoop, calls=%fused_computation.34 | loop fusion | flops 20971520 | bytes 62914560 | tf_op jit(solution)/shard_map/div | solution.py:80
  73.2 6.2 pad_maximum_fusion
  79.4 26.7 %copy.146 = f32[4,32,128,128]{1,0,3,2:T(4,128)} copy(f32[4,32,128,128]{2,3,1,0:T(8,128)} %pad_maximum_fusion) | data formatting | bytes 16777216 | tf_op jit(solution)/shard_map/reshape | solution.py:130
  106.1 41.7 %reshape.77 = f32[4,1,524288]{2,1,0:T(1,128)} reshape(f32[16384,4,32]{2,1,0:T(4,128)} %bitcast.139) | data formatting | bytes 16777216
  147.8 5.8 all-to-all-start
  156.2 175.7 %all-to-all-done = f32[4,1,524288]{2,1,0:T(1,128)} async-done(((f32[4,1,524288]{2,1,0:T(1,128)}), f32[4,1,524288]{2,1,0:T(1,128)}, u32[]{:S(2)}, u32[]{:S(2)}) %all-to-all-start) | async-done | bytes 8388640 | tf_op jit(solution)/shard_map/all_to_all | solution.py:133
  332.4 28.4 %reduce = f32[4,524288]{1,0:T(4,128)} reduce(f32[4,1,524288]{2,1,0:T(1,128)} %all-to-all-done, f32[]{:T(128)} %broadcast.190), dimensions={1}, to_apply=%all_to_all.22.reduce_sub_computation | reduce | bytes 16777220 | tf_op jit(solution)/shard_map/all_to_all | solution.py:133
  360.8 47.7 %reshape.78 = f32[16384,4,32]{2,1,0:T(4,128)} reshape(f32[4,524288]{1,0:T(4,128)} %reduce) | data formatting | bytes 16777216
  408.6 28.8 %copy.147 = f32[4,32,4,4096]{3,2,1,0:T(4,128)} copy(f32[4,32,4,4096]{1,0,3,2:T(4,128)} %bitcast.140) | data formatting | bytes 16777216 | tf_op jit(solution)/shard_map/all_to_all | solution.py:133
  437.4 4.0 fusion.174
  441.5 2.4 copy.77
  443.9 6.8 fusion.50
  450.7 2.6 copy.80
  453.4 6.8 fusion.46
  460.2 7.3 fusion.9
  467.5 3.7 fusion.48
  471.1 7.0 fusion.6
  478.2 3.7 fusion.44
  481.8 3.7 fusion.3
  485.5 4.1 fusion.1
  489.6 3.8 pad_maximum_fusion.1
  493.4 10.3 %copy.91 = f32[4,128,4096]{2,0,1:T(4,128)} copy(f32[4,128,4096]{1,2,0:T(8,128)} %pad_maximum_fusion.1) | data formatting | bytes 16777216 | tf_op jit(solution)/shard_map/concatenate | solution.py:111
  503.7 188.6 %all_to_all.30 = f32[4,128,4096]{2,0,1:T(4,128)S(1)} all-to-all(f32[4,128,4096]{2,0,1:T(4,128)} %copy.91), channel_id=1, replica_groups=mesh['parts'=2,'tm'=4,'rows'=2,'cols'=2] {'tm'}, dimensions={1} | all-to-all | bytes 16777216 | tf_op jit(solution)/shard_map/all_to_all | solution.py:138
  692.3 4.9 copy.92
  697.1 2.8 fusion.173
  699.9 4.7 copy.96
  704.6 6.1 slice.107
  710.7 10.3 %fusion.61 = f32[2,32,128,128]{3,2,1,0:T(8,128)} fusion(f32[2,32,128,128]{3,2,1,0:T(8,128)} %slice.107), kind=kOutput, calls=%fused_computation.94 | convolution fusion | flops 1610842112 | bytes 8388608 | tf_op jit(solution)/shard_map/au,cnuv->cnav/dot_general | solution.py:57
  721.0 8.6 %fusion.55 = f32[2,32,128,128]{3,2,1,0:T(8,128)} fusion(f32[2,32,128,128]{3,2,1,0:T(8,128)S(1)} %copy-done), kind=kOutput, calls=%fused_computation.88 | convolution fusion | flops 1610842112 | bytes 8388608 | tf_op jit(solution)/shard_map/au,cnuv->cnav/dot_general | solution.py:54
  729.7 4.7 copy.93
  734.4 6.1 slice.105
  740.4 9.3 %fusion.53 = f32[2,32,128,128]{3,2,1,0:T(8,128)S(1)} fusion(f32[2,32,128,128]{3,2,1,0:T(8,128)} %slice.105), kind=kOutput, calls=%fused_computation.86 | convolution fusion | flops 1610842112 | bytes 8388608 | tf_op jit(solution)/shard_map/au,cnuv->cnav/dot_general | solution.py:57
  749.7 7.0 fusion.63
  756.8 4.3 fusion.24
  761.1 4.9 multiply_bitcast_fusion.2
  768.3 5.6 copy.106
  (28 shorter events, 12.9 us)
Async XLA Ops:
  3.2 14.5 %copy-start.2 = (bf16[32,128,256]{1,2,0:T(8,128)(2,1)}, bf16[32,128,256]{1,2,0:T(8,128)(2,1)S(1)}, u32[]{:S(2)}) copy-start(bf16[32,128,256]{1,2,0:T(8,128)(2,1)S(1)} %copy.61) | copy-start | bytes 6291460
  5.5 12.2 %copy-start.5 = (bf16[32,128,128]{1,2,0:T(8,128)(2,1)}, bf16[32,128,128]{1,2,0:T(8,128)(2,1)S(1)}, u32[]{:S(2)}) copy-start(bf16[32,128,128]{1,2,0:T(8,128)(2,1)S(1)} %copy.62) | copy-start | bytes 3145732
  5.5 7.7 collective-permute-start
  8.7 7.4 collective-permute-start.1
  45.7 4.4 copy-start.3
  45.7 4.4 copy-start.6
  147.8 184.1 %all-to-all-start = ((f32[4,1,524288]{2,1,0:T(1,128)}), f32[4,1,524288]{2,1,0:T(1,128)}, u32[]{:S(2)}, u32[]{:S(2)}) async-start(f32[4,1,524288]{2,1,0:T(1,128)} %reshape.77), calls=%async_computation | async-start | bytes 16777216 | tf_op jit(solution)/shard_map/all_to_all | solution.py:133
  710.7 10.4 %copy-start = (f32[2,32,128,128]{3,2,1,0:T(8,128)S(1)}, f32[2,32,128,128]{3,2,1,0:T(8,128)}, u32[]{:S(2)}) copy-start(f32[2,32,128,128]{3,2,1,0:T(8,128)} %slice.107) | copy-start | bytes 12582916
  721.0 8.7 %copy-start.8 = (f32[2,32,4,4096]{3,1,2,0:T(8,128)S(1)}, f32[2,32,4,4096]{3,1,2,0:T(8,128)}, u32[]{:S(2)}) copy-start(f32[2,32,4,4096]{3,1,2,0:T(8,128)} %get-tuple-element.7) | copy-start | bytes 12582916
  740.4 9.3 %copy-start.1 = (f32[2,32,128,128]{3,2,1,0:T(8,128)S(1)}, f32[2,32,128,128]{3,2,1,0:T(8,128)}, u32[]{:S(2)}) copy-start(f32[2,32,128,128]{3,2,1,0:T(8,128)} %slice.105) | copy-start | bytes 12582916
  749.7 7.1 copy-start.4
  756.8 4.4 copy-start.7
where the time goes:
time: 790 us; the launch traced here: 774 us
  local copies, waits for them, and re-layouts  211 us (27%)
  blocking collectives  189 us (24%)
  waiting for transfers between devices  181 us (23%)
  matrix products  117 us (15%)
  other arithmetic  64.9 us (8%)
  starting transfers between devices  11.1 us (1%)
    all_to_all x1, blocking collectives, on_device(): lax.all_to_all(filtered, 'tm', split_axis=1, concat_axis=2, tiled=True)  189 us
    all_to_all x1, waiting for transfers between devices, on_device(): lax.all_to_all(payload, 'tm', split_axis=2, concat_axis=1, tiled=True)  176 us
    unnamed x22, local copies, waits for them, and re-layouts  94.9 us
    all_to_all x2, local copies, waits for them, and re-layouts, on_device(): lax.all_to_all(payload, 'tm', split_axis=2, concat_axis=1, tiled=True)  29.4 us
    all_to_all x1, other arithmetic, on_device(): lax.all_to_all(payload, 'tm', split_axis=2, concat_axis=1, tiled=True)  28.4 us
    reshape x1, local copies, waits for them, and re-layouts, on_device(): jnp.concatenate([joined_real, joined_imag], axis=0)  26.7 us
  transfers between devices with their start and end apart: 3, of which 3 were waited for; matrix products, arithmetic and copies ran while one was open for 0% of the time, Pallas kernels for 0%

commit v1 on v0

--- a/solution.py
+++ b/solution.py
@@ -1,11 +1,465 @@
+import functools
 import math
 
 import jax
 import jax.numpy as jnp
+import ml_dtypes
+import numpy as np
 from jax import lax
+from jax.experimental import pallas as pl
+from jax.experimental.pallas import tpu as pltpu
 from jax.sharding import PartitionSpec as P
 
 noise_level = 0.05
+f32 = jnp.float32
+bf16 = jnp.bfloat16
+i16 = jnp.int16
+TOP = 32766.0
+STEPS = 256.0
+TINY = 1e-30
+VMEM_BYTES = 56 * 1024 * 1024
+
+
+def real_basis(length, cosines_first):
+    half = length // 2
+    place = np.arange(length, dtype=np.int64)
+    wave = np.arange(half + 1, dtype=np.int64)
+    angles = (wave[:, None] * place[None, :] % length) * (2.0 * np.pi / length)
+    cosines = np.cos(angles) * math.sqrt(2.0 / length)
+    cosines[0] /= math.sqrt(2.0)
+    cosines[half] /= math.sqrt(2.0)
+    sines = np.sin(angles[1:half]) * math.sqrt(2.0 / length)
+    return np.concatenate([cosines, sines], axis=0)
+
+
+def split_table(table):
+    high = table.astype(np.float32).astype(ml_dtypes.bfloat16)
+    low = (table - high.astype(np.float64)).astype(np.float32).astype(ml_dtypes.bfloat16)
+    return high, low
+
+
+def left_split(table):
+    high, low = split_table(table)
+    return np.block([[high, high], [low, np.zeros_like(low)]])
+
+
+def right_split(table):
+    high, low = split_table(table)
+    return np.block([[high, low], [high, np.zeros_like(low)]])
+
+
+def band(length, reach):
+    place = np.arange(length)
+    near = (np.abs(place[:, None] - place[None, :]) <= reach).astype(np.float32)
+    near = near.astype(ml_dtypes.bfloat16)
+    return np.concatenate([near, near], axis=1)
+
+
+def lane_choices(side):
+    half = side // 2
+    picks = np.zeros((side, 2 * side), np.float32)
+    for lane in range(side):
+        wave = half if lane == half else lane % half
+        picks[wave, lane] = 1.0
+        picks[wave if wave in (0, half) else side - wave, side + lane] = 1.0
+    return picks.astype(ml_dtypes.bfloat16)
+
+
+def dot(a, b):
+    return jnp.dot(a, b, preferred_element_type=f32)
+
+
+def pieces(x, axis):
+    high = x.astype(bf16)
+    low = (x - high.astype(f32)).astype(bf16)
+    return jnp.concatenate([high, low], axis=axis)
+
+
+def halves_sum(x, axis):
+    size = x.shape[axis] // 2
+    if axis == 0:
+        return x[:size] + x[size:]
+    return x[:, :size] + x[:, size:]
+
+
+def special_lanes(shape, side):
+    lane = lax.broadcasted_iota(jnp.int32, shape, len(shape) - 1) % side
+    return (lane == 0) | (lane == side // 2)
+
+
+def lane_signs(shape, side):
+    lane = lax.broadcasted_iota(jnp.int32, shape, len(shape) - 1) % side
+    return jnp.where(lane < side // 2, -1.0, 1.0).astype(f32)
+
+
+def code_of(top):
+    return jnp.ceil(jnp.log2(jnp.maximum(top, TINY)) * STEPS)
+
+
+def prep_kernel(n, transfer_ref, *refs):
+    outs, held = refs[:n], refs[n]
+    count, side, _ = transfer_ref.shape
+    half = side // 2
+    groups = half // n
+    me, core = lax.axis_index("tm"), lax.axis_index("cols")
+
+    def fill(t, carry):
+        held[pl.ds(pl.multiple_of(t * side, side), side), :] = transfer_ref[t].astype(f32)
+        return carry
+
+    lax.fori_loop(0, count, fill, 0)
+    for shift in range(n):
+        dest = lax.rem(me + shift, n)
+        for j in range(groups):
+            g = dest * groups + j
+            minus = jnp.where(g == 0, half, side - g)
+            row = jnp.where(core == 0, g, minus)
+            outs[shift][j] = held[pl.ds(row, count, stride=side), :].astype(bf16)
+
+
+def weight_kernel(n, cutoff_ref, picks_ref, band_ref, *refs):
+    mine, theirs = refs[:n], refs[n : 2 * n]
+    weight_ref, inverse_ref, kept_ref, rows, cuts = refs[2 * n :]
+    groups, count, side = mine[0].shape
+    half = side // 2
+    time_len = n * count
+    me, core = lax.axis_index("tm"), lax.axis_index("cols")
+    for shift in range(n):
+        source = lax.rem(me + n - shift, n)
+        at = pl.ds(pl.multiple_of(source * count, count), count)
+        for j in range(groups):
+            rows[core, j, at, :] = mine[shift][j]
+            rows[1 - core, j, at, :] = theirs[shift][j]
+    picks = picks_ref[...]
+    flipped = jnp.concatenate([picks[:, side:], picks[:, :side]], axis=1)
+    for j in range(groups):
+        g = me * groups + j
+        cuts[0, pl.ds(j, 1), :] = cutoff_ref[pl.ds(g, 1), :].astype(f32)
+        cuts[1, pl.ds(j, 1), :] = cutoff_ref[
+            pl.ds(jnp.where(g == 0, half, side - g), 1), :
+        ].astype(f32)
+
+    def arrange(plus, minus, first):
+        a, c = plus[:, :side], plus[:, side:]
+        b, d = minus[:, :side], minus[:, side:]
+        early = jnp.concatenate([a, jnp.where(first, d, c)], axis=1)
+        late = jnp.concatenate([jnp.where(first, c, b), jnp.where(first, b, d)], axis=1)
+        return early, late
+
+    cut_plus = dot(cuts[0].astype(bf16), picks)
+    cut_minus = dot(cuts[1].astype(bf16), flipped)
+    row = lax.broadcasted_iota(jnp.int32, (groups, side), 0)
+    early, late = arrange(cut_plus, cut_minus, (row == 0) & (me == 0))
+    kept_ref[0] = early
+    kept_ref[1] = late
+
+    def one(j, carry):
+        plus = dot(rows[0, j], picks)
+        minus = dot(rows[1, j], flipped)
+        first = jnp.full((time_len, side), me * groups + j) == 0
+        for order, weight in enumerate(arrange(plus, minus, first)):
+            weight_ref[j, order] = weight.astype(bf16)
+            total = dot(band_ref[...], pieces(weight * weight, 0))
+            inverse_ref[j, order] = 1.0 / (total + noise_level)
+        return carry
+
+    lax.fori_loop(0, groups, one, 0)
+
+
+def quantize_rows(values_ref, tops_ref, out_ref, series, count, side):
+    codes = code_of(tops_ref[...])
+    out_ref[series * count :, :] = codes.astype(jnp.int32).astype(i16)
+    tops_ref[...] = jnp.exp2(codes * (-1.0 / STEPS)) * TOP
+
+    def one(j, carry):
+        scaled = values_ref[j] * tops_ref[pl.ds(j, 1), :]
+        at = pl.ds(pl.multiple_of(j * count, count), count)
+        out_ref[at, :] = jnp.round(scaled).astype(jnp.int32).astype(i16)
+        return carry
+
+    lax.fori_loop(0, series, one, 0, unroll=4)
+
+
+def scales_of(in_ref, series, count):
+    codes = in_ref[series * count :, :].astype(jnp.int32).astype(f32)
+    return jnp.exp2(codes * (1.0 / STEPS)) * (1.0 / TOP)
+
+
+def forward_kernel(n, frames_ref, left_ref, right_ref, *refs):
+    outs, spectra, values, tops = refs[:n], *refs[n:]
+    count, side, _ = frames_ref.shape
+    half = side // 2
+    groups = half // n
+    series = 2 * groups
+    me = lax.axis_index("tm")
+
+    def transform(pair, carry):
+        t = pair * 2
+        both = jnp.concatenate([frames_ref[t], frames_ref[t + 1]], axis=1)
+        rows = halves_sum(dot(left_ref[...], both), 0)
+        for k in range(2):
+            split = pieces(rows[:, k * side : (k + 1) * side], 1)
+            at = pl.ds(pl.multiple_of((t + k) * side, side), side)
+            spectra[at, :] = halves_sum(dot(split, right_ref[...]), 1)
+        return carry
+
+    lax.fori_loop(0, count // 2, transform, 0, unroll=2)
+    single = special_lanes((count, side), side)
+    signs = lane_signs((count, side), side)
+    for shift in range(n):
+        dest = lax.rem(me + shift, n)
+
+        def butterfly(j, carry):
+            g = dest * groups + j
+            even = spectra[pl.ds(g, count, stride=side), :]
+            odd = spectra[pl.ds(half + g, count, stride=side), :]
+            mixed = pltpu.roll(odd, half, 1) * signs
+            alone = single | (jnp.full((count, side), g) == 0)
+            first = even + jnp.where(alone, 0.0, mixed)
+            second = jnp.where(alone, odd, even - mixed)
+            values[j] = first
+            values[groups + j] = second
+            tops[pl.ds(j, 1), :] = jnp.max(jnp.abs(first), axis=0, keepdims=True)
+            tops[pl.ds(groups + j, 1), :] = jnp.max(jnp.abs(second), axis=0, keepdims=True)
+            return carry
+
+        lax.fori_loop(0, groups, butterfly, 0, unroll=2)
+        quantize_rows(values, tops, outs[shift], series, count, side)
+
+
+def filter_kernel(n, weight_ref, inverse_ref, kept_ref, band_ref, time_ref, back_ref, *refs):
+    ins, outs = refs[:n], refs[n : 2 * n]
+    scales, joined, values, tops = refs[2 * n :]
+    groups, _, time_len, wide = weight_ref.shape
+    side = wide // 2
+    count = time_len // n
+    series = 2 * groups
+    me = lax.axis_index("tm")
+    for shift in range(n):
+        scales[shift] = scales_of(ins[shift], series, count)
+    row = lax.broadcasted_iota(jnp.int32, (time_len, wide), 0)
+    distance = jnp.where(row <= time_len // 2, row, row - time_len // 2).astype(f32)
+
+    def one(j, carry):
+        for shift in range(n):
+            source = lax.rem(me + n - shift, n)
+            at = pl.ds(pl.multiple_of(source * count, count), count)
+            for k in range(2):
+                s = k * groups + j
+                part = ins[shift][pl.ds(pl.multiple_of(s * count, count), count), :]
+                part = part.astype(jnp.int32).astype(f32) * scales[shift, pl.ds(s, 1), :]
+                joined[at, k * side : (k + 1) * side] = part
+        spectra = joined[...]
+        total = None
+        for order in range(2):
+            terms = weight_ref[j, order].astype(f32) * spectra
+            ratio = dot(band_ref[...], pieces(terms, 0)) * inverse_ref[j, order]
+            coefficients = halves_sum(dot(time_ref[...], pieces(ratio, 0)), 0)
+            keep = distance <= kept_ref[order, pl.ds(j, 1), :]
+            coefficients = jnp.where(keep, coefficients, 0.0)
+            total = coefficients if total is None else total + coefficients
+        back = halves_sum(dot(back_ref[...], pieces(total, 0)), 0)
+        joined[...] = back
+        for shift in range(n):
+            dest = lax.rem(me + shift, n)
+            at = pl.ds(pl.multiple_of(dest * count, count), count)
+            for k in range(2):
+                s = k * groups + j
+                part = joined[at, k * side : (k + 1) * side]
+                values[shift, s] = part
+                tops[shift, pl.ds(s, 1), :] = jnp.max(jnp.abs(part), axis=0, keepdims=True)
+        return carry
+
+    lax.fori_loop(0, groups, one, 0)
+    for shift in range(n):
+        quantize_rows(values.at[shift], tops.at[shift], outs[shift], series, count, side)
+
+
+def inverse_kernel(n, aliased, left_ref, right_ref, *refs):
+    ins, refs = refs[:n], refs[n:]
+    if aliased:
+        refs = refs[1:]
+    out_ref, scales, packed, rows = refs
+    count, side, _ = out_ref.shape
+    half = side // 2
+    groups = half // n
+    series = 2 * groups
+    me = lax.axis_index("tm")
+    single = special_lanes((count, side), side)
+    signs = -lane_signs((count, side), side)
+    for shift in range(n):
+        dest = lax.rem(me + n - shift, n)
+        scales[...] = scales_of(ins[shift], series, count)
+
+        def butterfly(j, carry):
+            g = dest * groups + j
+            parts = []
+            for k in range(2):
+                s = k * groups + j
+                part = ins[shift][pl.ds(pl.multiple_of(s * count, count), count), :]
+                parts.append(part.astype(jnp.int32).astype(f32) * scales[pl.ds(s, 1), :])
+            first, second = parts
+            alone = single | (jnp.full((count, side), g) == 0)
+            mixed = pltpu.roll((first - second) * 0.5, half, 1) * signs
+            even = jnp.where(alone, first, (first + second) * 0.5)
+            odd = jnp.where(alone, second, mixed)
+            packed[pl.ds(pl.multiple_of(j * count, count), count), :] = pieces(even, 1)
+            packed[pl.ds(pl.multiple_of((groups + j) * count, count), count), :] = pieces(odd, 1)
+            return carry
+
+        lax.fori_loop(0, groups, butterfly, 0, unroll=2)
+        for k in range(2):
+            size = groups * count
+            done = halves_sum(dot(packed[k * size : (k + 1) * size, :], right_ref[...]), 1)
+            start = (k * half + dest * groups) * count
+            rows[pl.ds(pl.multiple_of(start, size), size), :] = done
+
+    def transform(pair, carry):
+        t = pair * 2
+        both = jnp.concatenate(
+            [
+                rows[pl.ds(t, side, stride=count), :],
+                rows[pl.ds(t + 1, side, stride=count), :],
+            ],
+            axis=1,
+        )
+        done = halves_sum(dot(left_ref[...], pieces(both, 0)), 0)
+        out_ref[t] = done[:, :side]
+        out_ref[t + 1] = done[:, side:]
+        return carry
+
+    lax.fori_loop(0, count // 2, transform, 0, unroll=2)
+
+
+def params():
+    return pltpu.CompilerParams(vmem_limit_bytes=VMEM_BYTES)
+
+
+def cost(flops, size):
+    return pl.CostEstimate(flops=int(flops), bytes_accessed=int(size), transcendentals=0)
+
+
+def shifted(block, axis, n, shift):
+    if shift == 0:
+        return block
+    return lax.ppermute(block, axis, [(k, (k + shift) % n) for k in range(n)])
+
+
+def on_device_fast(n, frames, transfer, cutoff):
+    count, side = frames.shape[0], transfer.shape[1]
+    across = frames.shape[2] // side
+    half = side // 2
+    groups = half // n
+    series = 2 * groups
+    time_len = n * count
+    space = real_basis(side, False)
+    clock = real_basis(time_len, True)
+    spatial_left = jnp.asarray(np.concatenate(split_table(space), axis=0))
+    spatial_right = jnp.asarray(right_split(space.T))
+    inverse_left = jnp.asarray(left_split(space.T))
+    inverse_right = jnp.asarray(right_split(space))
+    time_left = jnp.asarray(left_split(clock))
+    back_left = jnp.asarray(left_split(0.5 * clock.T))
+    banded = jnp.asarray(band(time_len, 2))
+    picks = jnp.asarray(lane_choices(side))
+    block = jax.ShapeDtypeStruct((series * count + series, side), i16)
+    sds = jax.ShapeDtypeStruct
+
+    shares = pl.pallas_call(
+        functools.partial(prep_kernel, n),
+        out_shape=[sds((groups, count, side), bf16)] * n,
+        scratch_shapes=[pltpu.VMEM((count * side, side), f32)],
+        compiler_params=params(),
+        cost_estimate=cost(0, 4 * transfer.size),
+        name="prep",
+    )(transfer)
+    mine = [shifted(shares[s], "tm", n, s) for s in range(n)]
+    theirs = [lax.ppermute(share, "cols", [(0, 1), (1, 0)]) for share in mine]
+
+    received = []
+    for channel in range(across):
+        blocks = pl.pallas_call(
+            functools.partial(forward_kernel, n),
+            out_shape=[block] * n,
+            grid=(1,),
+            in_specs=[
+                pl.BlockSpec((count, side, side), lambda _, c=channel: (0, 0, c)),
+                pl.BlockSpec(spatial_left.shape, lambda _: (0, 0)),
+                pl.BlockSpec(spatial_right.shape, lambda _: (0, 0)),
+            ],
+            out_specs=[pl.BlockSpec(block.shape, lambda _: (0, 0))] * n,
+            scratch_shapes=[
+                pltpu.VMEM((count * side, side), f32),
+                pltpu.VMEM((series, count, side), f32),
+                pltpu.VMEM((series, side), f32),
+            ],
+            compiler_params=params(),
+            cost_estimate=cost(count * side**3 * 12, count * side * side * 8),
+            name="forward",
+        )(frames, spatial_left, spatial_right)
+        received.append([shifted(blocks[s], "tm", n, s) for s in range(n)])
+
+    weight, inverse, kept = pl.pallas_call(
+        functools.partial(weight_kernel, n),
+        out_shape=[
+            sds((groups, 2, time_len, 2 * side), bf16),
+            sds((groups, 2, time_len, 2 * side), f32),
+            sds((2, groups, 2 * side), f32),
+        ],
+        scratch_shapes=[
+            pltpu.VMEM((2, groups, time_len, side), bf16),
+            pltpu.VMEM((2, groups, side), f32),
+        ],
+        compiler_params=params(),
+        cost_estimate=cost(groups * time_len * side * side * 24, groups * time_len * side * 28),
+        name="weights",
+    )(cutoff, picks, banded, *mine, *theirs)
+
+    returned = []
+    for channel in range(across):
+        blocks = pl.pallas_call(
+            functools.partial(filter_kernel, n),
+            out_shape=[block] * n,
+            scratch_shapes=[
+                pltpu.VMEM((n, series, side), f32),
+                pltpu.VMEM((time_len, 2 * side), f32),
+                pltpu.VMEM((n, series, count, side), f32),
+                pltpu.VMEM((n, series, side), f32),
+            ],
+            compiler_params=params(),
+            cost_estimate=cost(groups * time_len**2 * side * 80, groups * time_len * side * 40),
+            name="filter",
+        )(weight, inverse, kept, banded, time_left, back_left, *received[channel])
+        returned.append([shifted(blocks[s], "tm", n, s) for s in range(n)])
+
+    restored = None
+    for channel in range(across):
+        aliased = restored is not None
+        operands = [inverse_left, inverse_right, *returned[channel]]
+        in_specs = [
+            pl.BlockSpec(inverse_left.shape, lambda _: (0, 0)),
+            pl.BlockSpec(inverse_right.shape, lambda _: (0, 0)),
+        ] + [pl.BlockSpec(block.shape, lambda _: (0, 0))] * n
+        if aliased:
+            operands.append(restored)
+            in_specs.append(pl.BlockSpec(memory_space=pl.ANY))
+        restored = pl.pallas_call(
+            functools.partial(inverse_kernel, n, aliased),
+            out_shape=sds((count, side, across * side), f32),
+            grid=(1,),
+            in_specs=in_specs,
+            out_specs=pl.BlockSpec((count, side, side), lambda _, c=channel: (0, 0, c)),
+            scratch_shapes=[
+                pltpu.VMEM((series, side), f32),
+                pltpu.VMEM((series * count, 2 * side), bf16),
+                pltpu.VMEM((side * count, side), f32),
+            ],
+            input_output_aliases={len(operands) - 1: 0} if aliased else {},
+            compiler_params=params(),
+            cost_estimate=cost(count * side**3 * 14, count * side * side * 8),
+            name="inverse",
+        )(*operands)
+    return restored
 
 
 def with_halo(cells, sides, width):
@@ -116,7 +570,7 @@
     return images.reshape(total, side, across, side).transpose(2, 0, 1, 3)
 
 
-def on_device(frames, transfer, cutoff):
+def on_device_plain(frames, transfer, cutoff):
     count = frames.shape[0]
     side = transfer.shape[1]
     across = frames.shape[2] // side
@@ -141,6 +595,15 @@
     return result.transpose(1, 2, 0, 3).reshape(count, side, across * side)
 
 
+def on_device(frames, transfer, cutoff):
+    n = lax.axis_size("tm")
+    count, side = frames.shape[0], transfer.shape[1]
+    tiled = side == 128 and frames.shape[1] == side and count % 32 == 0 and (n * count) % 128 == 0
+    if tiled and lax.axis_size("cols") == 2 and (side // 2) % n == 0 and side // n % 32 == 0:
+        return on_device_fast(n, frames, transfer, cutoff)
+    return on_device_plain(frames, transfer, cutoff)
+
+
 def solution(mesh):
     return jax.shard_map(
         on_device,

time: 790 us -> 140 us (0.18); the launches traced: 774 us -> 139 us
  local copies, waits for them, and re-layouts: 211 us -> 2.96 us
  blocking collectives: 189 us -> 0 us
  waiting for transfers between devices: 181 us -> 24.7 us
  matrix products: 117 us -> 0 us
  Pallas kernels: 0 us -> 82.2 us
  other arithmetic: 64.9 us -> 0 us
  starting transfers between devices: 11.1 us -> 29.3 us
    all_to_all x1 -> x0, blocking collectives: 189 us -> none  [on_device(): lax.all_to_all(filtered, 'tm', split_axis=1, concat_axis=2, tiled=True)]
    all_to_all x1 -> x0, waiting for transfers between devices: 176 us -> none  [on_device(): lax.all_to_all(payload, 'tm', split_axis=2, concat_axis=1, tiled=True)]
    dot_general x20 -> x0, matrix products: 117 us -> none  [the longest x1 10.3 us: inverse_spatial(): jnp.einsum('au,cnuv->cnav', cos_space, spec_imag, precision=highest)]
    unnamed x22 -> x38, local copies, waits for them, and re-layouts: 94.9 us -> 2.96 us
    pallas_call x0 -> x8, Pallas kernels: none -> 82.2 us  [the longest x2 31.1 us: on_device_fast(): pl.pallas_call(functools.partial(filter_kernel, n), out_shape=[block] * n...]
    reshape x3 -> x0, local copies, waits for them, and re-layouts: 35.3 us -> none  [the longest x1 26.7 us: on_device(): jnp.concatenate([joined_real, joined_imag], axis=0)]
    all_to_all x3 -> x0, local copies, waits for them, and re-layouts: 34.2 us -> none  [the longest x2 29.4 us: on_device(): lax.all_to_all(payload, 'tm', split_axis=2, concat_axis=1, tiled=True)]
    slice x8 -> x0, local copies, waits for them, and re-layouts: 33.4 us -> none  [the longest x3 13.5 us: on_device(): spectra_back[:across]]
  transfers between devices with their start and end apart: 3 -> 19, of which waited for: 3 -> 3; matrix products, arithmetic and copies ran while one was open for 0% -> 0% of each run, Pallas kernels for 0% -> 50%
where the time goes in v1:
time: 140 us; the launch traced here: 139 us
  Pallas kernels  82.2 us (59%)
  starting transfers between devices  29.3 us (21%)
  waiting for transfers between devices  24.7 us (18%)
  local copies, waits for them, and re-layouts  2.96 us (2%)
    pallas_call x2, Pallas kernels, on_device_fast(): pl.pallas_call(functools.partial(filter_kernel, n), out_shape=[block] * n...  31.1 us
    ppermute x15, waiting for transfers between devices, shifted(): return lax.ppermute(block, axis, [(k, (k + shift) % n) for k in range(n)])  24.7 us
    ppermute x15, starting transfers between devices, shifted(): return lax.ppermute(block, axis, [(k, (k + shift) % n) for k in range(n)])  20.3 us
    pallas_call x2, Pallas kernels, on_device_fast(): pl.pallas_call(functools.partial(inverse_kernel, n, aliased), out_shape=s...  19.3 us
    pallas_call x2, Pallas kernels, on_device_fast(): pl.pallas_call(functools.partial(forward_kernel, n), out_shape=[block] *...  18.7 us
    pallas_call x1, Pallas kernels, on_device_fast(): pl.pallas_call(functools.partial(weight_kernel, n), out_shape=[sds((group...  9.84 us
    ppermute x4, starting transfers between devices, on_device_fast(): theirs = [lax.ppermute(share, 'cols', [(0, 1), (1, 0)]) for share in mine]  8.99 us
    pallas_call x1, Pallas kernels, on_device_fast(): pl.pallas_call(functools.partial(prep_kernel, n), out_shape=[sds((groups,...  3.3 us
  transfers between devices with their start and end apart: 19, of which 3 were waited for; matrix products, arithmetic and copies ran while one was open for 0% of the time, Pallas kernels for 50%

profile of v1, /device:TPU:13, one launch (start us, length us, event | category | flops | bytes accessed | tf_op | source)
XLA Modules:
  0.0 139.4 jit_solution(8256376689402838797)
XLA Ops:
  0.0 3.3 %prep.1 = (bf16[16,32,128]{2,1,0:T(8,128)(2,1)}, bf16[16,32,128]{2,1,0:T(8,128)(2,1)}, bf16[16,32,128]{2,1,0:T(8,128)(2,1)}, bf16[16,32,128]{2,1,0:T(8,128)(2,1)}) custom-call(bf16[32,128,128]{2,1,0:T(8,128)(2,1)} %transfer_ref.1), custom_call_target="tpu_custom_call" | custom-call | bytes 2097152 | tf_op jit(solution)/shard_map/prep/pallas_call | solution.py:368
  3.3 1.3 collective-permute-start
  4.6 1.0 collective-permute-start.1
  5.6 1.5 %collective-permute-start.2 = (bf16[16,32,128]{2,1,0:T(8,128)(2,1)}, bf16[16,32,128]{2,1,0:T(8,128)(2,1)S(1)}, u32[]{:S(2)}, u32[]{:S(2)}) collective-permute-start(bf16[16,32,128]{2,1,0:T(8,128)(2,1)} %get-tuple-element.31), channel_id=1, source_target_pairs={{0,12},{4,0},{8,4},{12,8},{1,13},{5,1},{9,5},{13,9},{2,14},{6,2},{... | collective-permute-start | bytes 393224 | tf_op jit(solution)/shard_map/ppermute | solution.py:345
  7.1 1.5 %collective-permute-start.3 = (bf16[16,32,128]{2,1,0:T(8,128)(2,1)}, bf16[16,32,128]{2,1,0:T(8,128)(2,1)S(1)}, u32[]{:S(2)}, u32[]{:S(2)}) collective-permute-start(bf16[16,32,128]{2,1,0:T(8,128)(2,1)} %get-tuple-element.28.refs_0_), channel_id=1, source_target_pairs={{0,1},{1,0},{2,3},{3,2},{4,5},{5,4},{6,7},{7,6},{8,9},{9,8},{10,11... | collective-permute-start | bytes 393224 | tf_op jit(solution)/shard_map/ppermute | solution.py:377
  8.6 0.0 collective-permute-done.refs_1_
  8.6 6.8 %collective-permute-start.4 = (bf16[16,32,128]{2,1,0:T(8,128)(2,1)S(1)}, bf16[16,32,128]{2,1,0:T(8,128)(2,1)S(1)}, u32[]{:S(2)}, u32[]{:S(2)}) collective-permute-start(bf16[16,32,128]{2,1,0:T(8,128)(2,1)S(1)} %collective-permute-done.refs_1_), channel_id=1, source_target_pairs={{0,1},{1,0},{2,3},{3,2},{4,5},{5,4},{6,7},{7,6},{8,9},{9,8},{10,11... | collective-permute-start | bytes 393224 | tf_op jit(solution)/shard_map/ppermute | solution.py:377
  15.4 9.4 %forward.3 = (s16[1056,128]{1,0:T(8,128)(2,1)}, s16[1056,128]{1,0:T(8,128)(2,1)}, s16[1056,128]{1,0:T(8,128)(2,1)}, s16[1056,128]{1,0:T(8,128)(2,1)}) custom-call(bf16[32,128,256]{2,1,0:T(8,128)(2,1)} %frames_ref.3, bf16[256,128]{1,0:T(8,128)(2,1)} %constant.16.clone.left_ref, bf16[256,256]{1,0:T(8,128)(2,1)} %constant.17.clone.right_ref), custom_call_target="tpu_custom_call" | custom-call | flops 805306368 | bytes 4194304 | tf_op jit(solution)/shard_map/forward/pallas_call | solution.py:381
  24.7 2.1 %collective-permute-start.13 = (s16[1056,128]{1,0:T(8,128)(2,1)}, s16[1056,128]{1,0:T(8,128)(2,1)S(1)}, u32[]{:S(2)}, u32[]{:S(2)}) collective-permute-start(s16[1056,128]{1,0:T(8,128)(2,1)} %get-tuple-element.44), channel_id=1, source_target_pairs={{0,4},{4,8},{8,12},{12,0},{1,5},{5,9},{9,13},{13,1},{2,6},{6,10},{... | collective-permute-start | bytes 811016 | tf_op jit(solution)/shard_map/ppermute | solution.py:345
  26.8 0.0 collective-permute-done.1.refs_2_
  26.8 0.0 collective-permute-start.14
  26.8 0.0 collective-permute-done.2.refs_3_
  26.9 1.2 collective-permute-start.15
  28.1 0.0 collective-permute-done.3.refs_4_
  28.1 0.6 collective-permute-start.5
  28.7 0.0 collective-permute-done.4.refs_5_
  28.7 0.1 collective-permute-start.6
  28.8 9.3 %forward.2 = (s16[1056,128]{1,0:T(8,128)(2,1)}, s16[1056,128]{1,0:T(8,128)(2,1)}, s16[1056,128]{1,0:T(8,128)(2,1)}, s16[1056,128]{1,0:T(8,128)(2,1)}) custom-call(bf16[32,128,256]{2,1,0:T(8,128)(2,1)} %frames_ref.3, bf16[256,128]{1,0:T(8,128)(2,1)} %constant.16.clone.left_ref, bf16[256,256]{1,0:T(8,128)(2,1)} %constant.17.clone.right_ref), custom_call_target="tpu_custom_call" | custom-call | flops 805306368 | bytes 4194304 | tf_op jit(solution)/shard_map/forward/pallas_call | solution.py:381
  38.1 0.0 collective-permute-done.5.refs_6_
  38.1 0.3 collective-permute-start.7
  38.4 0.0 collective-permute-done.6.refs_7_
  38.4 4.4 %collective-permute-start.8 = (s16[1056,128]{1,0:T(8,128)(2,1)}, s16[1056,128]{1,0:T(8,128)(2,1)S(1)}, u32[]{:S(2)}, u32[]{:S(2)}) collective-permute-start(s16[1056,128]{1,0:T(8,128)(2,1)} %get-tuple-element.37), channel_id=1, source_target_pairs={{0,8},{4,12},{8,0},{12,4},{1,9},{5,13},{9,1},{13,5},{2,10},{6,14},... | collective-permute-start | bytes 811016 | tf_op jit(solution)/shard_map/ppermute | solution.py:345
  42.8 9.8 %weights.1 = (bf16[16,2,128,256]{3,2,1,0:T(8,128)(2,1)}, f32[16,2,128,256]{3,2,1,0:T(8,128)}, f32[2,16,256]{2,1,0:T(8,128)}) custom-call(s32[128,128]{1,0:T(8,128)} %cutoff_ref.1, bf16[128,256]{1,0:T(8,128)(2,1)} %constant.23.clone.picks_ref, bf16[128,256]{1,0:T(8,128)(2,1)} %constant.22.clone.band_ref, bf16[16,32,128]{2,1,0:T(8,128)(2,1)} %get-tuple-element.28.refs_0_, ...), custom_call_target="tpu_custom_call" | custom-call | flops 805306368 | bytes 7340032 | tf_op jit(solution)/shard_map/weights/pallas_call | solution.py:402
  52.7 0.0 collective-permute-done.13.refs_1_
  52.7 0.1 collective-permute-start.9
  52.8 0.0 collective-permute-done.14.refs_2_
  52.8 7.4 %collective-permute-done.15.refs_3_ = s16[1056,128]{1,0:T(8,128)(2,1)S(1)} collective-permute-done((s16[1056,128]{1,0:T(8,128)(2,1)}, s16[1056,128]{1,0:T(8,128)(2,1)S(1)}, u32[]{:S(2)}, u32[]{:S(2)}) %collective-permute-start.15) | collective-permute-done | bytes 270368 | tf_op jit(solution)/shard_map/ppermute | solution.py:345
  60.2 0.7 copy-done.10
  60.9 15.5 %filter.3 = (s16[1056,128]{1,0:T(8,128)(2,1)}, s16[1056,128]{1,0:T(8,128)(2,1)}, s16[1056,128]{1,0:T(8,128)(2,1)}, s16[1056,128]{1,0:T(8,128)(2,1)}) custom-call(bf16[16,2,128,256]{3,2,1,0:T(8,128)(2,1)} %get-tuple-element.32.weight_ref, f32[16,2,128,256]{3,2,1,0:T(8,128)} %get-tuple-element.33.inverse_ref, f32[2,16,256]{2,1,0:T(8,128)} %get-tuple-element.34.kept_ref, ...), custom_call_target="tpu_custom_call" | custom-call | flops 2684354560 | bytes 10485760 | tf_op jit(solution)/shard_map/filter/pallas_call | solution.py:420
  76.4 0.0 collective-permute-start.16
  76.4 4.9 %collective-permute-start.17 = (s16[1056,128]{1,0:T(8,128)(2,1)}, s16[1056,128]{1,0:T(8,128)(2,1)S(1)}, u32[]{:S(2)}, u32[]{:S(2)}) collective-permute-start(s16[1056,128]{1,0:T(8,128)(2,1)} %get-tuple-element.49), channel_id=1, source_target_pairs={{0,8},{4,12},{8,0},{12,4},{1,9},{5,13},{9,1},{13,5},{2,10},{6,14},... | collective-permute-start | bytes 811016 | tf_op jit(solution)/shard_map/ppermute | solution.py:345
  81.3 0.0 collective-permute-done.7.refs_1_
  81.3 1.4 %collective-permute-start.18 = (s16[1056,128]{1,0:T(8,128)(2,1)}, s16[1056,128]{1,0:T(8,128)(2,1)S(1)}, u32[]{:S(2)}, u32[]{:S(2)}) collective-permute-start(s16[1056,128]{1,0:T(8,128)(2,1)} %get-tuple-element.50), channel_id=1, source_target_pairs={{0,12},{4,0},{8,4},{12,8},{1,13},{5,1},{9,5},{13,9},{2,14},{6,2},{... | collective-permute-start | bytes 811016 | tf_op jit(solution)/shard_map/ppermute | solution.py:345
  82.7 0.0 collective-permute-done.8.refs_2_
  82.8 0.7 copy-done.9
  83.4 0.1 copy-done.11
  83.5 15.6 %filter.2 = (s16[1056,128]{1,0:T(8,128)(2,1)}, s16[1056,128]{1,0:T(8,128)(2,1)}, s16[1056,128]{1,0:T(8,128)(2,1)}, s16[1056,128]{1,0:T(8,128)(2,1)}) custom-call(bf16[16,2,128,256]{3,2,1,0:T(8,128)(2,1)} %get-tuple-element.32.weight_ref, f32[16,2,128,256]{3,2,1,0:T(8,128)} %get-tuple-element.33.inverse_ref, f32[2,16,256]{2,1,0:T(8,128)} %get-tuple-element.34.kept_ref, ...), custom_call_target="tpu_custom_call" | custom-call | flops 2684354560 | bytes 10485760 | tf_op jit(solution)/shard_map/filter/pallas_call | solution.py:420
  99.1 0.1 collective-permute-start.10
  99.2 2.1 %collective-permute-start.11 = (s16[1056,128]{1,0:T(8,128)(2,1)}, s16[1056,128]{1,0:T(8,128)(2,1)S(1)}, u32[]{:S(2)}, u32[]{:S(2)}) collective-permute-start(s16[1056,128]{1,0:T(8,128)(2,1)} %get-tuple-element.41), channel_id=1, source_target_pairs={{0,8},{4,12},{8,0},{12,4},{1,9},{5,13},{9,1},{13,5},{2,10},{6,14},... | collective-permute-start | bytes 811016 | tf_op jit(solution)/shard_map/ppermute | solution.py:345
  101.3 0.0 collective-permute-done.16.refs_1_
  101.3 0.0 collective-permute-start.12
  101.3 16.1 %collective-permute-done.18.refs_3_ = s16[1056,128]{1,0:T(8,128)(2,1)S(1)} collective-permute-done((s16[1056,128]{1,0:T(8,128)(2,1)}, s16[1056,128]{1,0:T(8,128)(2,1)S(1)}, u32[]{:S(2)}, u32[]{:S(2)}) %collective-permute-start.18) | collective-permute-done | bytes 270368 | tf_op jit(solution)/shard_map/ppermute | solution.py:345
  117.4 0.7 copy-done.5
  118.1 9.7 %inverse.2.refs_4_ = f32[32,128,256]{2,1,0:T(8,128)} custom-call(bf16[256,256]{1,0:T(8,128)(2,1)} %constant.18.clone.left_ref, bf16[256,256]{1,0:T(8,128)(2,1)} %constant.19.clone.right_ref, s16[1056,128]{1,0:T(8,128)(2,1)} %get-tuple-element.47.refs_0_, s16[1056,128]{1,0:T(8,128)(2,1)} %copy-done.3, s16[1056,128]{1,0:T(8,128)(2,1)} %copy-done.4, ...), custom_call_target="tpu_custom_call" | custom-call | flops 939524096 | bytes 4194304 | tf_op jit(solution)/shard_map/inverse/pallas_call | solution.py:446
  127.8 0.0 collective-permute-done.11.refs_2_
  127.8 1.2 collective-permute-done.12.refs_3_
  129.0 0.7 copy-done.2
  129.7 9.7 %inverse.3 = f32[32,128,256]{2,1,0:T(8,128)} custom-call(bf16[256,256]{1,0:T(8,128)(2,1)} %constant.18.clone.left_ref, bf16[256,256]{1,0:T(8,128)(2,1)} %constant.19.clone.right_ref, s16[1056,128]{1,0:T(8,128)(2,1)} %get-tuple-element.39.refs_0_, s16[1056,128]{1,0:T(8,128)(2,1)} %copy-done, ...), custom_call_target="tpu_custom_call", output_to_operand_aliasing={{}: (6, {})} | custom-call | flops 939524096 | bytes 4194304 | tf_op jit(solution)/shard_map/inverse/pallas_call | solution.py:446
  (36 shorter events, 0.1 us)
Async XLA Ops:
  3.3 5.3 %collective-permute-start = (bf16[16,32,128]{2,1,0:T(8,128)(2,1)}, bf16[16,32,128]{2,1,0:T(8,128)(2,1)S(1)}, u32[]{:S(2)}, u32[]{:S(2)}) collective-permute-start(bf16[16,32,128]{2,1,0:T(8,128)(2,1)} %get-tuple-element.29), channel_id=1, source_target_pairs={{0,4},{4,8},{8,12},{12,0},{1,5},{5,9},{9,13},{13,1},{2,6},{6,10},{... | collective-permute-start | bytes 393224 | tf_op jit(solution)/shard_map/ppermute | solution.py:345
  4.6 22.2 %collective-permute-start.1 = (bf16[16,32,128]{2,1,0:T(8,128)(2,1)}, bf16[16,32,128]{2,1,0:T(8,128)(2,1)S(1)}, u32[]{:S(2)}, u32[]{:S(2)}) collective-permute-start(bf16[16,32,128]{2,1,0:T(8,128)(2,1)} %get-tuple-element.30), channel_id=1, source_target_pairs={{0,8},{4,12},{8,0},{12,4},{1,9},{5,13},{9,1},{13,5},{2,10},{6,14},... | collective-permute-start | bytes 393224 | tf_op jit(solution)/shard_map/ppermute | solution.py:345
  5.6 21.2 %collective-permute-start.2 = (bf16[16,32,128]{2,1,0:T(8,128)(2,1)}, bf16[16,32,128]{2,1,0:T(8,128)(2,1)S(1)}, u32[]{:S(2)}, u32[]{:S(2)}) collective-permute-start(bf16[16,32,128]{2,1,0:T(8,128)(2,1)} %get-tuple-element.31), channel_id=1, source_target_pairs={{0,12},{4,0},{8,4},{12,8},{1,13},{5,1},{9,5},{13,9},{2,14},{6,2},{... | collective-permute-start | bytes 393224 | tf_op jit(solution)/shard_map/ppermute | solution.py:345
  7.1 21.0 %collective-permute-start.3 = (bf16[16,32,128]{2,1,0:T(8,128)(2,1)}, bf16[16,32,128]{2,1,0:T(8,128)(2,1)S(1)}, u32[]{:S(2)}, u32[]{:S(2)}) collective-permute-start(bf16[16,32,128]{2,1,0:T(8,128)(2,1)} %get-tuple-element.28.refs_0_), channel_id=1, source_target_pairs={{0,1},{1,0},{2,3},{3,2},{4,5},{5,4},{6,7},{7,6},{8,9},{9,8},{10,11... | collective-permute-start | bytes 393224 | tf_op jit(solution)/shard_map/ppermute | solution.py:377
  8.6 34.2 %copy-start.12 = (bf16[16,32,128]{2,1,0:T(8,128)(2,1)}, bf16[16,32,128]{2,1,0:T(8,128)(2,1)S(1)}, u32[]{:S(2)}) copy-start(bf16[16,32,128]{2,1,0:T(8,128)(2,1)S(1)} %collective-permute-done.refs_1_) | copy-start | bytes 393220
  8.6 20.1 %collective-permute-start.4 = (bf16[16,32,128]{2,1,0:T(8,128)(2,1)S(1)}, bf16[16,32,128]{2,1,0:T(8,128)(2,1)S(1)}, u32[]{:S(2)}, u32[]{:S(2)}) collective-permute-start(bf16[16,32,128]{2,1,0:T(8,128)(2,1)S(1)} %collective-permute-done.refs_1_), channel_id=1, source_target_pairs={{0,1},{1,0},{2,3},{3,2},{4,5},{5,4},{6,7},{7,6},{8,9},{9,8},{10,11... | collective-permute-start | bytes 393224 | tf_op jit(solution)/shard_map/ppermute | solution.py:377
  24.7 28.0 %collective-permute-start.13 = (s16[1056,128]{1,0:T(8,128)(2,1)}, s16[1056,128]{1,0:T(8,128)(2,1)S(1)}, u32[]{:S(2)}, u32[]{:S(2)}) collective-permute-start(s16[1056,128]{1,0:T(8,128)(2,1)} %get-tuple-element.44), channel_id=1, source_target_pairs={{0,4},{4,8},{8,12},{12,0},{1,5},{5,9},{9,13},{13,1},{2,6},{6,10},{... | collective-permute-start | bytes 811016 | tf_op jit(solution)/shard_map/ppermute | solution.py:345
  26.8 16.0 %copy-start.13 = (bf16[16,32,128]{2,1,0:T(8,128)(2,1)}, bf16[16,32,128]{2,1,0:T(8,128)(2,1)S(1)}, u32[]{:S(2)}) copy-start(bf16[16,32,128]{2,1,0:T(8,128)(2,1)S(1)} %collective-permute-done.1.refs_2_) | copy-start | bytes 393220
  26.8 25.9 %collective-permute-start.14 = (s16[1056,128]{1,0:T(8,128)(2,1)}, s16[1056,128]{1,0:T(8,128)(2,1)S(1)}, u32[]{:S(2)}, u32[]{:S(2)}) collective-permute-start(s16[1056,128]{1,0:T(8,128)(2,1)} %get-tuple-element.45), channel_id=1, source_target_pairs={{0,8},{4,12},{8,0},{12,4},{1,9},{5,13},{9,1},{13,5},{2,10},{6,14},... | collective-permute-start | bytes 811016 | tf_op jit(solution)/shard_map/ppermute | solution.py:345
  26.8 16.0 %copy-start.14 = (bf16[16,32,128]{2,1,0:T(8,128)(2,1)}, bf16[16,32,128]{2,1,0:T(8,128)(2,1)S(1)}, u32[]{:S(2)}) copy-start(bf16[16,32,128]{2,1,0:T(8,128)(2,1)S(1)} %collective-permute-done.2.refs_3_) | copy-start | bytes 393220
  26.9 33.3 %collective-permute-start.15 = (s16[1056,128]{1,0:T(8,128)(2,1)}, s16[1056,128]{1,0:T(8,128)(2,1)S(1)}, u32[]{:S(2)}, u32[]{:S(2)}) collective-permute-start(s16[1056,128]{1,0:T(8,128)(2,1)} %get-tuple-element.46), channel_id=1, source_target_pairs={{0,12},{4,0},{8,4},{12,8},{1,13},{5,1},{9,5},{13,9},{2,14},{6,2},{... | collective-permute-start | bytes 811016 | tf_op jit(solution)/shard_map/ppermute | solution.py:345
  28.1 14.7 %copy-start.15 = (bf16[16,32,128]{2,1,0:T(8,128)(2,1)}, bf16[16,32,128]{2,1,0:T(8,128)(2,1)S(1)}, u32[]{:S(2)}) copy-start(bf16[16,32,128]{2,1,0:T(8,128)(2,1)S(1)} %collective-permute-done.3.refs_4_) | copy-start | bytes 393220
  28.1 10.0 %collective-permute-start.5 = (bf16[16,32,128]{2,1,0:T(8,128)(2,1)S(1)}, bf16[16,32,128]{2,1,0:T(8,128)(2,1)S(1)}, u32[]{:S(2)}, u32[]{:S(2)}) collective-permute-start(bf16[16,32,128]{2,1,0:T(8,128)(2,1)S(1)} %collective-permute-done.1.refs_2_), channel_id=1, source_target_pairs={{0,1},{1,0},{2,3},{3,2},{4,5},{5,4},{6,7},{7,6},{8,9},{9,8},{10,11... | collective-permute-start | bytes 393224 | tf_op jit(solution)/shard_map/ppermute | solution.py:377
  28.7 14.1 %copy-start.16 = (bf16[16,32,128]{2,1,0:T(8,128)(2,1)}, bf16[16,32,128]{2,1,0:T(8,128)(2,1)S(1)}, u32[]{:S(2)}) copy-start(bf16[16,32,128]{2,1,0:T(8,128)(2,1)S(1)} %collective-permute-done.4.refs_5_) | copy-start | bytes 393220
  28.7 9.7 %collective-permute-start.6 = (bf16[16,32,128]{2,1,0:T(8,128)(2,1)S(1)}, bf16[16,32,128]{2,1,0:T(8,128)(2,1)S(1)}, u32[]{:S(2)}, u32[]{:S(2)}) collective-permute-start(bf16[16,32,128]{2,1,0:T(8,128)(2,1)S(1)} %collective-permute-done.2.refs_3_), channel_id=1, source_target_pairs={{0,1},{1,0},{2,3},{3,2},{4,5},{5,4},{6,7},{7,6},{8,9},{9,8},{10,11... | collective-permute-start | bytes 393224 | tf_op jit(solution)/shard_map/ppermute | solution.py:377
  38.1 4.7 %copy-start.17 = (bf16[16,32,128]{2,1,0:T(8,128)(2,1)}, bf16[16,32,128]{2,1,0:T(8,128)(2,1)S(1)}, u32[]{:S(2)}) copy-start(bf16[16,32,128]{2,1,0:T(8,128)(2,1)S(1)} %collective-permute-done.5.refs_6_) | copy-start | bytes 393220
  38.1 43.2 %collective-permute-start.7 = (s16[1056,128]{1,0:T(8,128)(2,1)}, s16[1056,128]{1,0:T(8,128)(2,1)S(1)}, u32[]{:S(2)}, u32[]{:S(2)}) collective-permute-start(s16[1056,128]{1,0:T(8,128)(2,1)} %get-tuple-element.36), channel_id=1, source_target_pairs={{0,4},{4,8},{8,12},{12,0},{1,5},{5,9},{9,13},{13,1},{2,6},{6,10},{... | collective-permute-start | bytes 811016 | tf_op jit(solution)/shard_map/ppermute | solution.py:345
  38.4 4.4 %copy-start.18 = (bf16[16,32,128]{2,1,0:T(8,128)(2,1)}, bf16[16,32,128]{2,1,0:T(8,128)(2,1)S(1)}, u32[]{:S(2)}) copy-start(bf16[16,32,128]{2,1,0:T(8,128)(2,1)S(1)} %collective-permute-done.6.refs_7_) | copy-start | bytes 393220
  38.4 44.3 %collective-permute-start.8 = (s16[1056,128]{1,0:T(8,128)(2,1)}, s16[1056,128]{1,0:T(8,128)(2,1)S(1)}, u32[]{:S(2)}, u32[]{:S(2)}) collective-permute-start(s16[1056,128]{1,0:T(8,128)(2,1)} %get-tuple-element.37), channel_id=1, source_target_pairs={{0,8},{4,12},{8,0},{12,4},{1,9},{5,13},{9,1},{13,5},{2,10},{6,14},... | collective-permute-start | bytes 811016 | tf_op jit(solution)/shard_map/ppermute | solution.py:345
  52.7 7.5 %copy-start.6 = (s16[1056,128]{1,0:T(8,128)(2,1)}, s16[1056,128]{1,0:T(8,128)(2,1)S(1)}, u32[]{:S(2)}) copy-start(s16[1056,128]{1,0:T(8,128)(2,1)S(1)} %collective-permute-done.13.refs_1_) | copy-start | bytes 811012
  52.7 30.0 %collective-permute-start.9 = (s16[1056,128]{1,0:T(8,128)(2,1)}, s16[1056,128]{1,0:T(8,128)(2,1)S(1)}, u32[]{:S(2)}, u32[]{:S(2)}) collective-permute-start(s16[1056,128]{1,0:T(8,128)(2,1)} %get-tuple-element.38), channel_id=1, source_target_pairs={{0,12},{4,0},{8,4},{12,8},{1,13},{5,1},{9,5},{13,9},{2,14},{6,2},{... | collective-permute-start | bytes 811016 | tf_op jit(solution)/shard_map/ppermute | solution.py:345
  52.8 7.4 %copy-start.7 = (s16[1056,128]{1,0:T(8,128)(2,1)}, s16[1056,128]{1,0:T(8,128)(2,1)S(1)}, u32[]{:S(2)}) copy-start(s16[1056,128]{1,0:T(8,128)(2,1)S(1)} %collective-permute-done.14.refs_2_) | copy-start | bytes 811012
  60.2 0.7 copy-start.10
  76.4 24.9 %collective-permute-start.16 = (s16[1056,128]{1,0:T(8,128)(2,1)}, s16[1056,128]{1,0:T(8,128)(2,1)S(1)}, u32[]{:S(2)}, u32[]{:S(2)}) collective-permute-start(s16[1056,128]{1,0:T(8,128)(2,1)} %get-tuple-element.48), channel_id=1, source_target_pairs={{0,4},{4,8},{8,12},{12,0},{1,5},{5,9},{9,13},{13,1},{2,6},{6,10},{... | collective-permute-start | bytes 811016 | tf_op jit(solution)/shard_map/ppermute | solution.py:345
  76.4 24.9 %collective-permute-start.17 = (s16[1056,128]{1,0:T(8,128)(2,1)}, s16[1056,128]{1,0:T(8,128)(2,1)S(1)}, u32[]{:S(2)}, u32[]{:S(2)}) collective-permute-start(s16[1056,128]{1,0:T(8,128)(2,1)} %get-tuple-element.49), channel_id=1, source_target_pairs={{0,8},{4,12},{8,0},{12,4},{1,9},{5,13},{9,1},{13,5},{2,10},{6,14},... | collective-permute-start | bytes 811016 | tf_op jit(solution)/shard_map/ppermute | solution.py:345
  81.3 1.5 %copy-start.8 = (s16[1056,128]{1,0:T(8,128)(2,1)}, s16[1056,128]{1,0:T(8,128)(2,1)S(1)}, u32[]{:S(2)}) copy-start(s16[1056,128]{1,0:T(8,128)(2,1)S(1)} %collective-permute-done.7.refs_1_) | copy-start | bytes 811012
  81.3 36.1 %collective-permute-start.18 = (s16[1056,128]{1,0:T(8,128)(2,1)}, s16[1056,128]{1,0:T(8,128)(2,1)S(1)}, u32[]{:S(2)}, u32[]{:S(2)}) collective-permute-start(s16[1056,128]{1,0:T(8,128)(2,1)} %get-tuple-element.50), channel_id=1, source_target_pairs={{0,12},{4,0},{8,4},{12,8},{1,13},{5,1},{9,5},{13,9},{2,14},{6,2},{... | collective-permute-start | bytes 811016 | tf_op jit(solution)/shard_map/ppermute | solution.py:345
  82.7 0.7 copy-start.9
  82.7 0.8 copy-start.11
  99.1 28.7 %collective-permute-start.10 = (s16[1056,128]{1,0:T(8,128)(2,1)}, s16[1056,128]{1,0:T(8,128)(2,1)S(1)}, u32[]{:S(2)}, u32[]{:S(2)}) collective-permute-start(s16[1056,128]{1,0:T(8,128)(2,1)} %get-tuple-element.40), channel_id=1, source_target_pairs={{0,4},{4,8},{8,12},{12,0},{1,5},{5,9},{9,13},{13,1},{2,6},{6,10},{... | collective-permute-start | bytes 811016 | tf_op jit(solution)/shard_map/ppermute | solution.py:345
  99.2 28.6 %collective-permute-start.11 = (s16[1056,128]{1,0:T(8,128)(2,1)}, s16[1056,128]{1,0:T(8,128)(2,1)S(1)}, u32[]{:S(2)}, u32[]{:S(2)}) collective-permute-start(s16[1056,128]{1,0:T(8,128)(2,1)} %get-tuple-element.41), channel_id=1, source_target_pairs={{0,8},{4,12},{8,0},{12,4},{1,9},{5,13},{9,1},{13,5},{2,10},{6,14},... | collective-permute-start | bytes 811016 | tf_op jit(solution)/shard_map/ppermute | solution.py:345
  101.3 16.1 %copy-start.3 = (s16[1056,128]{1,0:T(8,128)(2,1)}, s16[1056,128]{1,0:T(8,128)(2,1)S(1)}, u32[]{:S(2)}) copy-start(s16[1056,128]{1,0:T(8,128)(2,1)S(1)} %collective-permute-done.16.refs_1_) | copy-start | bytes 811012
  101.3 27.7 %collective-permute-start.12 = (s16[1056,128]{1,0:T(8,128)(2,1)}, s16[1056,128]{1,0:T(8,128)(2,1)S(1)}, u32[]{:S(2)}, u32[]{:S(2)}) collective-permute-start(s16[1056,128]{1,0:T(8,128)(2,1)} %get-tuple-element.42), channel_id=1, source_target_pairs={{0,12},{4,0},{8,4},{12,8},{1,13},{5,1},{9,5},{13,9},{2,14},{6,2},{... | collective-permute-start | bytes 811016 | tf_op jit(solution)/shard_map/ppermute | solution.py:345
  101.3 16.1 %copy-start.4 = (s16[1056,128]{1,0:T(8,128)(2,1)}, s16[1056,128]{1,0:T(8,128)(2,1)S(1)}, u32[]{:S(2)}) copy-start(s16[1056,128]{1,0:T(8,128)(2,1)S(1)} %collective-permute-done.17.refs_2_) | copy-start | bytes 811012
  117.4 0.7 copy-start.5
  127.8 1.2 copy-start
  127.8 1.2 copy-start.1
  129.0 0.7 copy-start.2
